TPU v7x, 256 devices: a whole 4x4x8 slice. The times are simulated.
256 devices in a mesh: ctx: 16 (over y, x), head: 4 (over z_lo, core), clip: 4 (over z_hi).
Axes of the slice: x: 4, y: 4, z: 8 (z_hi: 4, z_lo: 2; z = z_hi * 2 + z_lo), core: 2. Of those that a mesh axis runs over, the one named last changes fastest.
Arguments:
- queries: bfloat16 [4, 2048, 2560], P('clip', 'ctx', 'head'), may hold values from -40 to 40
- key_states: bfloat16 [4, 2048, 2560], P('clip', 'ctx', 'head'), may hold values from -40 to 40
- value_states: bfloat16 [4, 2048, 2560], P('clip', 'ctx', 'head'), may hold values from -40 to 40
- layer_grad: bfloat16 [4, 2048, 5120], P('clip', 'ctx'), may hold values from -6 to 6
- out_weight: bfloat16 [2560, 5120], P('head', 'clip'), may hold values from -0.125 to 0.125
- chosen: int32 [4, 32, 4], P('clip', 'ctx'), may hold values from 0 to 31, all different within a row
Outputs:
- attention: bfloat16 [4, 2048, 2560], P('clip', 'ctx', 'head')
- query_grad: bfloat16 [4, 2048, 2560], P('clip', 'ctx', 'head')
- key_grad: bfloat16 [4, 2048, 2560], P('clip', 'ctx', 'head')
- value_grad: bfloat16 [4, 2048, 2560], P('clip', 'ctx', 'head')
- weight_grad: bfloat16 [2560, 5120], P('head', 'clip')
Inputs may be any that keep to these rules, and one draw needn't show every extreme that they name: Each row names 4 different cubes of its clip; how often a key cube is chosen differs widely from cube to cube.
All inputs are finite; a program needn't handle non-finite values.
Results may differ from a plain program's by a relative error of at most 0.025.
Values may be sent and summed in bfloat16 or wider, within the bound.
No kernel may reach another device: no remote copies, remote signals or barrier semaphores. Data moves between devices by JAX's collectives and lax.ppermute only.
A program may use at most 128 MiB of HBM per device.

v0:
```python
import jax
import jax.numpy as jnp
from jax import lax
from jax.sharding import PartitionSpec as P

HD = 128
CUBE = 64


def cube_means(blocks):
    grouped = blocks.astype(jnp.float32).reshape(-1, CUBE, blocks.shape[-1])
    return jnp.mean(grouped, axis=1).astype(jnp.bfloat16)


def by_heads(blocks):
    return blocks.reshape(blocks.shape[0], -1, HD)


def softmax_rows(scores):
    largest = jnp.max(scores, axis=-1, keepdims=True)
    expons = jnp.exp(scores - largest)
    return expons / jnp.sum(expons, axis=-1, keepdims=True)


def on_device(queries, key_states, value_states, layer_grad, out_weight, chosen):
    scaling = HD ** (-0.5)
    query_local = queries[0]
    key_local = key_states[0]
    value_local = value_states[0]
    layer_local = layer_grad[0]
    picked = chosen[0]
    tok_local, width = query_local.shape
    heads_here = width // HD
    cubes_local = tok_local // CUBE
    picks_each = picked.shape[1]
    key_whole, value_whole = (
        lax.all_gather(key_local, "ctx", axis=0, tiled=True),
        lax.all_gather(value_local, "ctx", axis=0, tiled=True),
    )
    tok_whole = key_whole.shape[0]
    cubes_whole = tok_whole // CUBE
    query_cube = cube_means(query_local)
    key_cube, value_cube = (
        lax.all_gather(cube_means(key_local), "ctx", axis=0, tiled=True),
        lax.all_gather(cube_means(value_local), "ctx", axis=0, tiled=True),
    )
    qcube_heads = by_heads(query_cube)
    kcube_heads = by_heads(key_cube)
    vcube_heads = by_heads(value_cube)
    coarse_scores = (
        jnp.einsum("ahd,bhd->hab", qcube_heads, kcube_heads, preferred_element_type=jnp.float32)
        * scaling
    )
    coarse_p = softmax_rows(coarse_scores)
    coarse_half = coarse_p.astype(jnp.bfloat16)
    coarse_out = jnp.einsum(
        "hab,bhd->ahd", coarse_half, vcube_heads, preferred_element_type=jnp.float32
    )
    key_cubes = key_whole.reshape(cubes_whole, CUBE, width)
    value_cubes = value_whole.reshape(cubes_whole, CUBE, width)
    key_pick = key_cubes[picked].reshape(cubes_local, picks_each * CUBE, heads_here, HD)
    value_pick = value_cubes[picked].reshape(cubes_local, picks_each * CUBE, heads_here, HD)
    query_blocks = query_local.reshape(cubes_local, CUBE, heads_here, HD)
    fine_scores = (
        jnp.einsum("cthd,ckhd->chtk", query_blocks, key_pick, preferred_element_type=jnp.float32)
        * scaling
    )
    fine_p = softmax_rows(fine_scores)
    fine_half = fine_p.astype(jnp.bfloat16)
    fine_out = jnp.einsum(
        "chtk,ckhd->cthd", fine_half, value_pick, preferred_element_type=jnp.float32
    )
    attention = (
        (fine_out + coarse_out[:, None, :, :]).astype(jnp.bfloat16).reshape(tok_local, width)
    )
    attn_grad = lax.dot_general(
        layer_local,
        lax.all_gather(out_weight, "clip", axis=1, tiled=True),
        (((1,), (1,)), ((), ())),
        preferred_element_type=jnp.float32,
    ).astype(jnp.bfloat16)
    grad_cube = jnp.sum(
        attn_grad.astype(jnp.float32).reshape(cubes_local, CUBE, width), axis=1
    ).astype(jnp.bfloat16)
    gcube_heads = by_heads(grad_cube)
    coarse_dp = jnp.einsum(
        "ahd,bhd->hab", gcube_heads, vcube_heads, preferred_element_type=jnp.float32
    )
    coarse_delta = jnp.sum(coarse_p * coarse_dp, axis=-1, keepdims=True)
    coarse_ds = (scaling * coarse_p * (coarse_dp - coarse_delta)).astype(jnp.bfloat16)
    coarse_dq = jnp.einsum(
        "hab,bhd->ahd", coarse_ds, kcube_heads, preferred_element_type=jnp.float32
    )
    coarse_dk = jnp.einsum(
        "hab,ahd->bhd", coarse_ds, qcube_heads, preferred_element_type=jnp.float32
    )
    coarse_dv = jnp.einsum(
        "hab,ahd->bhd", coarse_half, gcube_heads, preferred_element_type=jnp.float32
    )
    cube_terms = (
        jnp.concatenate(
            [coarse_dk.reshape(cubes_whole, width), coarse_dv.reshape(cubes_whole, width)], axis=1
        )
        / CUBE
    )
    grad_blocks = attn_grad.reshape(cubes_local, CUBE, heads_here, HD)
    fine_dp = jnp.einsum(
        "cthd,ckhd->chtk", grad_blocks, value_pick, preferred_element_type=jnp.float32
    )
    fine_delta = jnp.sum(fine_p * fine_dp, axis=-1, keepdims=True)
    fine_ds = (scaling * fine_p * (fine_dp - fine_delta)).astype(jnp.bfloat16)
    query_grad = jnp.einsum(
        "chtk,ckhd->cthd", fine_ds, key_pick, preferred_element_type=jnp.float32
    )
    query_grad = (query_grad + coarse_dq[:, None, :, :] / CUBE).astype(jnp.bfloat16)
    query_grad = query_grad.reshape(tok_local, width)
    key_picked = jnp.einsum(
        "chtk,cthd->ckhd", fine_ds, query_blocks, preferred_element_type=jnp.float32
    )
    value_picked = jnp.einsum(
        "chtk,cthd->ckhd", fine_half, grad_blocks, preferred_element_type=jnp.float32
    )
    flat_terms = jnp.concatenate(
        [
            key_picked.reshape(cubes_local, picks_each, CUBE, width),
            value_picked.reshape(cubes_local, picks_each, CUBE, width),
        ],
        axis=3,
    )
    flat_terms = flat_terms.reshape(cubes_local * picks_each, CUBE, 2 * width)
    picked_flat = picked.reshape(-1)
    running = jnp.broadcast_to(cube_terms[:, None, :], (cubes_whole, CUBE, 2 * width))
    running = running.at[picked_flat].add(flat_terms)
    summed = lax.psum_scatter(
        running.reshape(tok_whole, 2 * width).astype(jnp.bfloat16),
        "ctx",
        scatter_dimension=0,
        tiled=True,
    ).astype(jnp.float32)
    key_grad = summed[:, :width].astype(jnp.bfloat16)
    value_grad = summed[:, width:].astype(jnp.bfloat16)
    weight_term = lax.dot_general(
        attention, layer_local, (((0,), (0,)), ((), ())), preferred_element_type=jnp.float32
    )
    over_clips = lax.psum_scatter(
        weight_term.astype(jnp.bfloat16), "clip", scatter_dimension=1, tiled=True
    )
    over_groups = lax.psum(over_clips, "ctx").astype(jnp.float32)
    weight_grad = over_groups.astype(jnp.bfloat16)
    return (attention[None], query_grad[None], key_grad[None], value_grad[None], weight_grad)


def solution(mesh):
    placed = (
        P("clip", "ctx", "head"),
        P("clip", "ctx", "head"),
        P("clip", "ctx", "head"),
        P("clip", "ctx", None),
        P("head", "clip"),
        P("clip", "ctx", None),
    )
    return jax.shard_map(
        on_device,
        mesh=mesh,
        in_specs=placed,
        out_specs=(
            P("clip", "ctx", "head"),
            P("clip", "ctx", "head"),
            P("clip", "ctx", "head"),
            P("clip", "ctx", "head"),
            P("head", "clip"),
        ),
        check_vma=False,
    )
```

profile of v0, /device:TPU:2, one launch (start us, length us, event | category | flops | bytes accessed | tf_op | source)
XLA Modules:
  0.0 575.4 jit_solution(13618390725349178365)
XLA Ops:
  7.2 0.0 all-gather.10.cloned.1.call-start
  7.2 0.7 all-gather.10.cloned.1.call-update
  7.9 0.0 all-gather.12.cloned.1.call-start
  8.0 0.7 all-gather.12.cloned.1.call-update
  8.7 0.0 all-gather.8.cloned.1.call-start
  8.7 0.7 all-gather.8.cloned.1.call-update
  9.4 0.0 reduce-scatter.5.cloned.1.call-start
  9.5 0.7 compare_select_fusion
  10.1 0.1 reshape.168
  10.2 1.0 convert_reduce_fusion.2
  11.2 23.5 %all-gather.2 = bf16[16,2,640]{2,1,0:T(2,128)(2,1)S(1)} all-gather(bf16[1,2,640]{2,1,0:T(2,128)(2,1)S(1)} %fusion.36), channel_id=1, replica_groups=mesh['ctx'=16,'head'=4,'clip'=4] {'ctx'}, dimensions={0}, use_global_device_ids=true | all-gather | bytes 43520 | tf_op jit(solution)/shard_map/all_gather | solution.py:45
  34.7 1.0 convert_reduce_fusion
  35.7 21.4 %all-gather.3 = bf16[16,2,640]{2,1,0:T(2,128)(2,1)S(1)} all-gather(bf16[1,2,640]{2,1,0:T(2,128)(2,1)S(1)} %fusion.38), channel_id=1, replica_groups=mesh['ctx'=16,'head'=4,'clip'=4] {'ctx'}, dimensions={0}, use_global_device_ids=true | all-gather | bytes 43520 | tf_op jit(solution)/shard_map/all_gather | solution.py:44
  57.1 0.2 reshape_squeeze.6
  57.4 0.3 fusion.46
  57.7 6.8 %all-gather.10.cloned.1.call-done = bf16[1,2048,640]{2,1,0:T(8,128)(2,1)} async-done(((bf16[1,128,640]{2,1,0:T(8,128)(2,1)}), bf16[1,2048,640]{2,1,0:T(8,128)(2,1)}) %all-gather.10.cloned.1.call-update) | async-done | bytes 2621456 | tf_op jit(solution)/shard_map/all_gather | solution.py:38
  64.5 2.4 gather_fusion
  66.9 1.7 reshape.154
  68.6 49.0 %all-gather.12.cloned.1.call-done = bf16[1,2048,640]{2,1,0:T(8,128)(2,1)} async-done(((bf16[1,128,640]{2,1,0:T(8,128)(2,1)}), bf16[1,2048,640]{2,1,0:T(8,128)(2,1)}) %all-gather.12.cloned.1.call-update) | async-done | bytes 2621456 | tf_op jit(solution)/shard_map/all_gather | solution.py:37
  117.6 2.4 gather_fusion.1
  120.0 0.7 reshape.156
  120.7 0.4 fusion.6
  121.1 1.0 fusion.47
  122.1 111.0 %all-gather.8.cloned.1.call-done = bf16[640,5120]{1,0:T(8,128)(2,1)} async-done(((bf16[640,1280]{1,0:T(8,128)(2,1)}), bf16[640,5120]{1,0:T(8,128)(2,1)}) %all-gather.8.cloned.1.call-update) | async-done | bytes 6553616 | tf_op jit(solution)/shard_map/all_gather | solution.py:78
  233.1 5.0 bitcast_reduce_fusion
  238.2 0.2 multiply_reduce_fusion.1
  238.4 0.1 convolution_bitcast_fusion.4
  238.5 2.4 fusion.14
  240.9 0.1 copy.70
  241.1 0.7 copy-done.4
  241.8 4.6 convolution_convert_fusion
  246.4 0.0 reduce-scatter.5.cloned.1.call-update
  246.4 0.2 reduce-scatter.3.cloned.1.call-start
  246.6 0.4 copy-done.12
  247.0 0.1 reshape_squeeze.7
  247.1 0.2 reshape.159
  247.3 0.7 copy-done.11
  248.1 2.4 convolution_bitcast_fusion
  250.5 2.0 copy.84
  252.4 1.4 concatenate.23
  253.8 2.0 multiply_reduce_fusion
  255.9 0.2 multiply_convert_fusion
  256.1 0.8 copy-done.8
  256.9 0.4 convolution_bitcast_fusion.1
  257.3 0.8 copy.82
  258.1 1.4 concatenate.22
  259.5 0.2 convolution_bitcast_fusion.2
  259.7 0.1 multiply_convert_fusion.1
  259.8 0.2 convolution_bitcast_fusion.3
  260.0 3.4 pad_maximum_fusion
  263.5 5.4 broadcast_in_dim.6
  268.9 5.7 scatter_fusion
  274.6 7.0 %convert_element_type.116 = bf16[32,64,1280]{2,1,0:T(8,128)(2,1)} convert(f32[32,64,1280]{2,1,0:T(8,128)} %scatter_fusion) | non-fusion elementwise | flops 2621440 | bytes 15728640 | tf_op jit(solution)/shard_map/convert_element_type | solution.py:135
  281.7 0.0 all-reduce.2.cloned.1.call-start
  281.7 97.3 %reduce-scatter.5.cloned.1.call-done = bf16[640,1280]{1,0:T(8,128)(2,1)} async-done(((bf16[640,5120]{1,0:T(8,128)(2,1)}), bf16[640,1280]{1,0:T(8,128)(2,1)}) %reduce-scatter.5.cloned.1.call-update) | async-done | bytes 1638416 | tf_op jit(solution)/shard_map/reduce_scatter | solution.py:145
  379.1 0.9 broadcast_in_dim_reshape.6
  379.9 0.1 fusion.17
  380.1 0.2 fusion.13
  380.3 0.1 copy.77
  380.5 0.9 broadcast_in_dim_reshape.7
  381.3 83.5 %reduce-scatter.3.cloned.1.call-done = bf16[128,1280]{1,0:T(8,128)(2,1)} async-done(((bf16[2048,1280]{1,0:T(8,128)(2,1)}), bf16[128,1280]{1,0:T(8,128)(2,1)}) %reduce-scatter.3.cloned.1.call-update) | async-done | bytes 327696 | tf_op jit(solution)/shard_map/reduce_scatter | solution.py:134
  464.8 1.7 slice_bitcast_fusion
  466.6 99.3 %all-reduce.2.cloned.1.call-done = bf16[640,1280]{1,0:T(8,128)(2,1)} async-done(((bf16[640,1280]{1,0:T(8,128)(2,1)}), bf16[640,1280]{1,0:T(8,128)(2,1)}) %all-reduce.2.cloned.1.call-update) | async-done | bytes 1638416 | tf_op jit(solution)/shard_map/psum | solution.py:148
  565.9 2.7 copy.129
  (35 shorter events, 0.3 us)
Async XLA Ops:
  7.2 226.0 %copy-start = (bf16[1,128,5120]{2,1,0:T(8,128)(2,1)S(1)}, bf16[1,128,5120]{2,1,0:T(8,128)(2,1)}, u32[]{:S(2)}) copy-start(bf16[1,128,5120]{2,1,0:T(8,128)(2,1)} %param.9) | copy-start | bytes 3932164
  7.2 49.9 %copy-start.10 = (bf16[1,128,640]{2,1,0:T(8,128)(2,1)S(1)}, bf16[1,128,640]{2,1,0:T(8,128)(2,1)}, u32[]{:S(2)}) copy-start(bf16[1,128,640]{2,1,0:T(8,128)(2,1)} %param.6) | copy-start | bytes 491524
  7.2 57.3 %all-gather.10.cloned.1.call-start = ((), (), s32[]{:S(2)}) async-start(), calls=%async_computation.6 | async-start | bytes 2785280 | tf_op jit(solution)/shard_map/all_gather | solution.py:38
  7.9 109.6 %all-gather.12.cloned.1.call-start = ((), (), s32[]{:S(2)}) async-start(), calls=%async_computation.7 | async-start | bytes 2785280 | tf_op jit(solution)/shard_map/all_gather | solution.py:37
  8.7 224.5 %all-gather.8.cloned.1.call-start = ((), (), s32[]{:S(2)}) async-start(), calls=%async_computation.2 | async-start | bytes 8192000 | tf_op jit(solution)/shard_map/all_gather | solution.py:78
  9.4 369.6 %reduce-scatter.5.cloned.1.call-start = ((), (), s32[]{:S(2)}) async-start(), calls=%async_computation.4 | async-start | bytes 8192000 | tf_op jit(solution)/shard_map/reduce_scatter | solution.py:145
  57.3 63.4 %copy-start.6 = (bf16[2,64,5,128]{3,2,1,0:T(8,128)(2,1)}, bf16[2,64,5,128]{3,2,1,0:T(8,128)(2,1)S(1)}, u32[]{:S(2)}) copy-start(bf16[2,64,5,128]{3,2,1,0:T(8,128)(2,1)S(1)} %reshape_squeeze.6) | copy-start | bytes 491524
  120.7 117.4 %copy-start.1 = (bf16[2,256,5,128]{3,2,1,0:T(8,128)(2,1)}, bf16[2,256,5,128]{3,2,1,0:T(8,128)(2,1)S(1)}, u32[]{:S(2)}) copy-start(bf16[2,256,5,128]{3,2,1,0:T(8,128)(2,1)S(1)} %reshape.156) | copy-start | bytes 1966084
  241.1 0.7 copy-start.4
  246.4 0.7 copy-start.12
  246.4 218.5 %reduce-scatter.3.cloned.1.call-start = ((), (), s32[]{:S(2)}) async-start(), calls=%async_computation.3 | async-start | bytes 5570560 | tf_op jit(solution)/shard_map/reduce_scatter | solution.py:134
  247.3 0.7 copy-start.11
  253.8 2.0 copy-start.3
  253.8 3.0 copy-start.7
  256.1 0.8 copy-start.8
  281.6 97.4 %copy-start.5 = (bf16[2,64,5,128]{3,2,1,0:T(8,128)(2,1)S(1)}, bf16[2,64,5,128]{3,2,1,0:T(8,128)(2,1)}, u32[]{:S(2)}) copy-start(bf16[2,64,5,128]{3,2,1,0:T(8,128)(2,1)} %copy-done.4) | copy-start | bytes 491524
  281.6 98.5 %copy-start.2 = (bf16[2,256,5,128]{3,2,1,0:T(8,128)(2,1)S(1)}, bf16[2,256,5,128]{3,2,1,0:T(8,128)(2,1)}, u32[]{:S(2)}) copy-start(bf16[2,256,5,128]{3,2,1,0:T(8,128)(2,1)} %copy-done.1) | copy-start | bytes 1966084
  281.6 98.5 %copy-start.9 = (bf16[2,5,64,256]{3,2,1,0:T(8,128)(2,1)S(1)}, bf16[2,5,64,256]{3,2,1,0:T(8,128)(2,1)}, u32[]{:S(2)}) copy-start(bf16[2,5,64,256]{3,2,1,0:T(8,128)(2,1)} %copy-done.8) | copy-start | bytes 983044
  281.7 284.2 %all-reduce.2.cloned.1.call-start = ((), (), s32[]{:S(2)}) async-start(), calls=%async_computation.5 | async-start | bytes 3276800 | tf_op jit(solution)/shard_map/psum | solution.py:148
Sparse Core Ops, SparseCore 0:
  10.5 53.9 all-gather.9
  66.9 50.6 all-gather.11
  119.4 113.7 all-gather.7
  246.5 132.4 reduce-scatter.4
  382.5 82.2 reduce-scatter.2
  468.1 97.7 all-reduce.1
where the time goes:
time: 576 us; the launch traced here: 575 us
  waiting for transfers between devices  449 us (78%)
  blocking collectives  44.9 us (8%)
  local copies, waits for them, and re-layouts  28 us (5%)
  other arithmetic  20.2 us (4%)
  matrix products  18.5 us (3%)
  between operations  14.4 us (2%)
    all_gather x1, waiting for transfers between devices, on_device(): lax.all_gather(out_weight, 'clip', axis=1, tiled=True)  111 us
    psum x1, waiting for transfers between devices, on_device(): over_groups = lax.psum(over_clips, 'ctx').astype(jnp.float32)  99.3 us
    reduce_scatter x1, waiting for transfers between devices, on_device(): lax.psum_scatter(weight_term.astype(jnp.bfloat16), 'clip', scatter_dimens...  97.3 us
    reduce_scatter x1, waiting for transfers between devices, on_device(): lax.psum_scatter(running.reshape(tok_whole, 2 * width).astype(jnp.bfloat1...  83.5 us
    all_gather x1, waiting for transfers between devices, on_device(): lax.all_gather(key_local, 'ctx', axis=0, tiled=True)  49 us
    all_gather x1, blocking collectives, on_device(): lax.all_gather(cube_means(value_local), 'ctx', axis=0, tiled=True)  23.5 us
    all_gather x1, blocking collectives, on_device(): lax.all_gather(cube_means(key_local), 'ctx', axis=0, tiled=True)  21.4 us
  transfers between devices with their start and end apart: 6, of which 6 were waited for; matrix products, arithmetic and copies ran while one was open for 8% of the time, Pallas kernels for 0%

commit v1 on v0

--- a/solution.py
+++ b/solution.py
@@ -1,10 +1,20 @@
+import functools
 import jax
 import jax.numpy as jnp
 from jax import lax
 from jax.sharding import PartitionSpec as P
+from jax.lax import all_gather
 
 HD = 128
 CUBE = 64
+
+
+def replace_view(xin, link_axis):
+    u1 = all_gather(xin, link_axis)
+    return jnp.sum(u1, axis=0)
+
+
+state_sources_all = functools.partial(replace_view, link_axis="ctx")
 
 
 def cube_means(blocks):
@@ -145,7 +155,7 @@
     over_clips = lax.psum_scatter(
         weight_term.astype(jnp.bfloat16), "clip", scatter_dimension=1, tiled=True
     )
-    over_groups = lax.psum(over_clips, "ctx").astype(jnp.float32)
+    over_groups = state_sources_all(over_clips).astype(jnp.float32)
     weight_grad = over_groups.astype(jnp.bfloat16)
     return (attention[None], query_grad[None], key_grad[None], value_grad[None], weight_grad)
 

time: 576 us -> 656 us (1.14)
  waiting for transfers between devices: 449 us -> 518 us
  other arithmetic: 20.2 us -> 37 us
    all_gather x0 -> x1, waiting for transfers between devices: none -> 165 us  [replace_view(): u1 = all_gather(xin, link_axis)]
    psum x1 -> x0, waiting for transfers between devices: 99.3 us -> none  [on_device(): over_groups = lax.psum(over_clips, 'ctx').astype(jnp.float32)]
    reduce_sum x0 -> x1, other arithmetic: none -> 16.8 us  [replace_view(): return jnp.sum(u1, axis=0)]
  transfers between devices with their start and end apart: 6 -> 6, of which waited for: 6 -> 6; matrix products, arithmetic and copies ran while one was open for 8% -> 7% of each run, Pallas kernels for 0% -> 0%
where the time goes in v1:
time: 656 us; the launch traced here: 655 us
  waiting for transfers between devices  518 us (79%)
  blocking collectives  44.9 us (7%)
  other arithmetic  37 us (6%)
  local copies, waits for them, and re-layouts  22.6 us (3%)
  matrix products  17.5 us (3%)
  between operations  14.4 us (2%)
    all_gather x1, waiting for transfers between devices, replace_view(): u1 = all_gather(xin, link_axis)  165 us
    all_gather x1, waiting for transfers between devices, on_device(): lax.all_gather(out_weight, 'clip', axis=1, tiled=True)  111 us
    reduce_scatter x1, waiting for transfers between devices, on_device(): lax.psum_scatter(weight_term.astype(jnp.bfloat16), 'clip', scatter_dimens...  101 us
    reduce_scatter x1, waiting for transfers between devices, on_device(): lax.psum_scatter(running.reshape(tok_whole, 2 * width).astype(jnp.bfloat1...  83.3 us
    all_gather x1, waiting for transfers between devices, on_device(): lax.all_gather(key_local, 'ctx', axis=0, tiled=True)  49 us
    all_gather x1, blocking collectives, on_device(): lax.all_gather(cube_means(value_local), 'ctx', axis=0, tiled=True)  23.5 us
    all_gather x1, blocking collectives, on_device(): lax.all_gather(cube_means(key_local), 'ctx', axis=0, tiled=True)  21.4 us
    reduce_sum x1, other arithmetic, replace_view(): return jnp.sum(u1, axis=0)  16.8 us
  transfers between devices with their start and end apart: 6, of which 6 were waited for; matrix products, arithmetic and copies ran while one was open for 7% of the time, Pallas kernels for 0%

profile of v1, /device:TPU:2, one launch (start us, length us, event | category | flops | bytes accessed | tf_op | source)
XLA Modules:
  0.0 654.8 jit_solution(6809979915041533690)
XLA Ops:
  7.2 0.0 all-gather.12.cloned.1.call-start
  7.2 0.7 all-gather.12.cloned.1.call-update
  7.9 0.0 all-gather.14.cloned.1.call-start
  8.0 0.7 all-gather.14.cloned.1.call-update
  8.7 0.0 all-gather.10.cloned.1.call-start
  8.7 0.7 all-gather.10.cloned.1.call-update
  9.4 0.0 reduce-scatter.5.cloned.1.call-start
  9.5 0.7 compare_select_fusion
  10.1 0.1 reshape.168
  10.2 1.0 convert_reduce_fusion.2
  11.2 23.5 %all-gather.3 = bf16[16,2,640]{2,1,0:T(2,128)(2,1)S(1)} all-gather(bf16[1,2,640]{2,1,0:T(2,128)(2,1)S(1)} %fusion.36), channel_id=1, replica_groups=mesh['ctx'=16,'head'=4,'clip'=4] {'ctx'}, dimensions={0}, use_global_device_ids=true | all-gather | bytes 43520 | tf_op jit(solution)/shard_map/all_gather | solution.py:55
  34.7 1.0 convert_reduce_fusion
  35.7 21.4 %all-gather.4 = bf16[16,2,640]{2,1,0:T(2,128)(2,1)S(1)} all-gather(bf16[1,2,640]{2,1,0:T(2,128)(2,1)S(1)} %fusion.38), channel_id=1, replica_groups=mesh['ctx'=16,'head'=4,'clip'=4] {'ctx'}, dimensions={0}, use_global_device_ids=true | all-gather | bytes 43520 | tf_op jit(solution)/shard_map/all_gather | solution.py:54
  57.1 0.2 reshape_squeeze.6
  57.4 0.3 fusion.46
  57.7 6.8 %all-gather.12.cloned.1.call-done = bf16[1,2048,640]{2,1,0:T(8,128)(2,1)} async-done(((bf16[1,128,640]{2,1,0:T(8,128)(2,1)}), bf16[1,2048,640]{2,1,0:T(8,128)(2,1)}) %all-gather.12.cloned.1.call-update) | async-done | bytes 2621456 | tf_op jit(solution)/shard_map/all_gather | solution.py:48
  64.5 2.4 gather_fusion
  66.9 1.7 reshape.154
  68.6 49.0 %all-gather.14.cloned.1.call-done = bf16[1,2048,640]{2,1,0:T(8,128)(2,1)} async-done(((bf16[1,128,640]{2,1,0:T(8,128)(2,1)}), bf16[1,2048,640]{2,1,0:T(8,128)(2,1)}) %all-gather.14.cloned.1.call-update) | async-done | bytes 2621456 | tf_op jit(solution)/shard_map/all_gather | solution.py:47
  117.6 2.4 gather_fusion.1
  120.0 0.7 reshape.156
  120.7 0.4 fusion.6
  121.1 1.0 fusion.47
  122.1 111.0 %all-gather.10.cloned.1.call-done = bf16[640,5120]{1,0:T(8,128)(2,1)} async-done(((bf16[640,1280]{1,0:T(8,128)(2,1)}), bf16[640,5120]{1,0:T(8,128)(2,1)}) %all-gather.10.cloned.1.call-update) | async-done | bytes 6553616 | tf_op jit(solution)/shard_map/all_gather | solution.py:88
  233.1 5.0 bitcast_reduce_fusion
  238.2 0.2 multiply_reduce_fusion.1
  238.4 0.1 convolution_bitcast_fusion.4
  238.5 2.4 fusion.14
  240.9 0.1 copy.70
  241.1 0.7 copy-done.5
  241.8 4.6 convolution_convert_fusion
  246.4 0.0 reduce-scatter.5.cloned.1.call-update
  246.4 0.2 reduce-scatter.3.cloned.1.call-start
  246.6 0.4 copy-done.13
  247.0 0.1 reshape_squeeze.7
  247.1 0.2 reshape.159
  247.3 0.7 copy-done.12
  248.0 1.3 convolution_bitcast_fusion
  249.4 1.0 copy.84
  250.4 0.4 concatenate.23
  250.8 2.0 multiply_reduce_fusion
  252.8 0.2 multiply_convert_fusion
  253.0 0.7 copy-done.9
  253.7 0.4 convolution_bitcast_fusion.1
  254.1 0.8 copy.82
  254.9 1.4 concatenate.22
  256.4 0.2 convolution_bitcast_fusion.2
  256.6 0.1 multiply_convert_fusion.1
  256.6 0.2 convolution_bitcast_fusion.3
  256.9 3.0 pad_maximum_fusion
  259.9 4.8 broadcast_in_dim.6
  264.7 6.0 scatter_fusion
  270.7 7.1 %convert_element_type.118 = bf16[32,64,1280]{2,1,0:T(8,128)(2,1)} convert(f32[32,64,1280]{2,1,0:T(8,128)} %scatter_fusion) | non-fusion elementwise | flops 2621440 | bytes 15728640 | tf_op jit(solution)/shard_map/convert_element_type | solution.py:145
  277.9 0.0 all-gather.16.cloned.1.call-start
  277.9 101.1 %reduce-scatter.5.cloned.1.call-done = bf16[640,1280]{1,0:T(8,128)(2,1)} async-done(((bf16[640,5120]{1,0:T(8,128)(2,1)}), bf16[640,1280]{1,0:T(8,128)(2,1)}) %reduce-scatter.5.cloned.1.call-update) | async-done | bytes 1638416 | tf_op jit(solution)/shard_map/reduce_scatter | solution.py:155
  379.1 0.9 broadcast_in_dim_reshape.6
  379.9 0.1 fusion.17
  380.1 0.2 fusion.13
  380.3 0.1 copy.77
  380.4 0.9 broadcast_in_dim_reshape.7
  381.3 83.3 %reduce-scatter.3.cloned.1.call-done = bf16[128,1280]{1,0:T(8,128)(2,1)} async-done(((bf16[2048,1280]{1,0:T(8,128)(2,1)}), bf16[128,1280]{1,0:T(8,128)(2,1)}) %reduce-scatter.3.cloned.1.call-update) | async-done | bytes 327696 | tf_op jit(solution)/shard_map/reduce_scatter | solution.py:144
  464.6 1.7 slice_bitcast_fusion
  466.4 164.7 %all-gather.16.cloned.1.call-done = bf16[10240,1280]{1,0:T(8,128)(2,1)} async-done(((bf16[640,1280]{1,0:T(8,128)(2,1)}), bf16[10240,1280]{1,0:T(8,128)(2,1)}) %all-gather.16.cloned.1.call-update) | async-done | bytes 26214416 | tf_op jit(solution)/shard_map/all_gather | solution.py:13
  631.1 16.8 %reduce_sum.92 = bf16[640,1280]{1,0:T(8,128)(2,1)} reduce(bf16[16,640,1280]{2,1,0:T(8,128)(2,1)} %bitcast.86, bf16[]{:T(256)} %constant.23.clone.1), dimensions={0}, to_apply=%region_13.0 | reduce | flops 12288000 | bytes 27852802 | tf_op jit(solution)/shard_map/reduce_sum | solution.py:14
  (37 shorter events, 0.3 us)
Async XLA Ops:
  7.2 226.0 %copy-start = (bf16[1,128,5120]{2,1,0:T(8,128)(2,1)S(1)}, bf16[1,128,5120]{2,1,0:T(8,128)(2,1)}, u32[]{:S(2)}) copy-start(bf16[1,128,5120]{2,1,0:T(8,128)(2,1)} %param.9) | copy-start | bytes 3932164
  7.2 49.9 %copy-start.11 = (bf16[1,128,640]{2,1,0:T(8,128)(2,1)S(1)}, bf16[1,128,640]{2,1,0:T(8,128)(2,1)}, u32[]{:S(2)}) copy-start(bf16[1,128,640]{2,1,0:T(8,128)(2,1)} %param.6) | copy-start | bytes 491524
  7.2 57.3 %all-gather.12.cloned.1.call-start = ((), (), s32[]{:S(2)}) async-start(), calls=%async_computation.5 | async-start | bytes 2785280 | tf_op jit(solution)/shard_map/all_gather | solution.py:48
  7.9 109.6 %all-gather.14.cloned.1.call-start = ((), (), s32[]{:S(2)}) async-start(), calls=%async_computation.6 | async-start | bytes 2785280 | tf_op jit(solution)/shard_map/all_gather | solution.py:47
  8.7 224.5 %all-gather.10.cloned.1.call-start = ((), (), s32[]{:S(2)}) async-start(), calls=%async_computation.2 | async-start | bytes 8192000 | tf_op jit(solution)/shard_map/all_gather | solution.py:88
  9.4 369.6 %reduce-scatter.5.cloned.1.call-start = ((), (), s32[]{:S(2)}) async-start(), calls=%async_computation.4 | async-start | bytes 8192000 | tf_op jit(solution)/shard_map/reduce_scatter | solution.py:155
  57.3 63.4 %copy-start.7 = (bf16[2,64,5,128]{3,2,1,0:T(8,128)(2,1)}, bf16[2,64,5,128]{3,2,1,0:T(8,128)(2,1)S(1)}, u32[]{:S(2)}) copy-start(bf16[2,64,5,128]{3,2,1,0:T(8,128)(2,1)S(1)} %reshape_squeeze.6) | copy-start | bytes 491524
  120.7 117.4 %copy-start.2 = (bf16[2,256,5,128]{3,2,1,0:T(8,128)(2,1)}, bf16[2,256,5,128]{3,2,1,0:T(8,128)(2,1)S(1)}, u32[]{:S(2)}) copy-start(bf16[2,256,5,128]{3,2,1,0:T(8,128)(2,1)S(1)} %reshape.156) | copy-start | bytes 1966084
  241.1 0.7 copy-start.5
  246.3 0.7 copy-start.13
  246.4 218.3 %reduce-scatter.3.cloned.1.call-start = ((), (), s32[]{:S(2)}) async-start(), calls=%async_computation.3 | async-start | bytes 5570560 | tf_op jit(solution)/shard_map/reduce_scatter | solution.py:144
  247.3 0.7 copy-start.12
  250.7 2.0 copy-start.4
  250.7 3.0 copy-start.8
  253.0 0.7 copy-start.9
  277.8 101.2 %copy-start.6 = (bf16[2,64,5,128]{3,2,1,0:T(8,128)(2,1)S(1)}, bf16[2,64,5,128]{3,2,1,0:T(8,128)(2,1)}, u32[]{:S(2)}) copy-start(bf16[2,64,5,128]{3,2,1,0:T(8,128)(2,1)} %copy-done.5) | copy-start | bytes 491524
  277.8 102.2 %copy-start.3 = (bf16[2,256,5,128]{3,2,1,0:T(8,128)(2,1)S(1)}, bf16[2,256,5,128]{3,2,1,0:T(8,128)(2,1)}, u32[]{:S(2)}) copy-start(bf16[2,256,5,128]{3,2,1,0:T(8,128)(2,1)} %copy-done.2) | copy-start | bytes 1966084
  277.8 102.2 %copy-start.10 = (bf16[2,5,64,256]{3,2,1,0:T(8,128)(2,1)S(1)}, bf16[2,5,64,256]{3,2,1,0:T(8,128)(2,1)}, u32[]{:S(2)}) copy-start(bf16[2,5,64,256]{3,2,1,0:T(8,128)(2,1)} %copy-done.9) | copy-start | bytes 983044
  277.9 353.3 %all-gather.16.cloned.1.call-start = ((), (), s32[]{:S(2)}) async-start(), calls=%async_computation.7 | async-start | bytes 27852800 | tf_op jit(solution)/shard_map/all_gather | solution.py:13
  631.1 16.8 %copy-start.1 = (bf16[1,128,5120]{2,1,0:T(8,128)(2,1)S(1)}, bf16[1,128,5120]{2,1,0:T(8,128)(2,1)}, u32[]{:S(2)}) copy-start(bf16[1,128,5120]{2,1,0:T(8,128)(2,1)} %param.9) | copy-start | bytes 3932164
Sparse Core Ops, SparseCore 0:
  10.5 53.9 all-gather.11
  66.9 50.6 all-gather.13
  119.4 113.7 all-gather.9
  246.5 132.4 reduce-scatter.4
  382.5 82.0 reduce-scatter.2
  466.9 164.1 all-gather.15
